TPU v7x, 256 devices: a whole 4x4x8 slice. The times are simulated.
256 devices in a mesh: tok: 32 (over x, y, core), tp: 8 (over z).
Axes of the slice: x: 4, y: 4, z: 8, core: 2. Of those that a mesh axis runs over, the one named last changes fastest.
Arguments:
- hidden: bfloat16 [2048, 7168], P('tok'), may hold values from -6 to 6
- ln_gain: float32 [7168], replicated, may hold values from 0.1 to 1.9
- ln_bias: float32 [7168], replicated, may hold values from -3 to 3
- w_qkv: bfloat16 [7168, 3, 7168], P('tok', None, 'tp'), may hold values from -0.0625 to 0.0625
- qkv_bias: float32 [3, 7168], P(None, 'tp'), may hold values from -3 to 3
- w_out: bfloat16 [7168, 7168], P('tp', 'tok'), may hold values from -0.0625 to 0.0625
- out_bias: float32 [7168], replicated, may hold values from -3 to 3
- dec_cache: bfloat16 [64, 1024, 2, 7168], P('tok', None, None, 'tp'), may hold values from -8 to 8
- prior_kv: bfloat16 [512, 2, 2, 7168], P('tok', None, None, 'tp'), may hold values from -8 to 8
- dec_len: int32 [64], P('tok'), may hold values from 1 to 1024, as said below
- offsets: int32 [2], replicated, may hold values from 4 to 512, as said below
Outputs:
- result: bfloat16 [2048, 7168], P('tok')
- new_kv: bfloat16 [2048, 2, 7168], P('tok', None, 'tp')
Inputs may be any that keep to these rules, and one draw needn't show every extreme that they name: `dec_len`: each decode request has 1 to 1024 cached positions; some request has exactly 1024. `offsets`: each prefill block follows 4 to 512 earlier positions; one of the two follows exactly 512.
All inputs are finite; a program needn't handle non-finite values.
Results may differ from a plain program's by a relative error of at most 0.015.
Values may be sent and summed in bfloat16 or wider, within the bound.
No kernel may reach another device: no remote copies, remote signals or barrier semaphores. Data moves between devices by JAX's collectives and lax.ppermute only.
A program may use at most 128 MiB of HBM per device.

v0:
```python
import jax
import jax.numpy as jnp
from jax import lax
from jax.sharding import PartitionSpec as P

HEAD = 128
WINDOW = 512
SINKS = 4
NEG = -1e30


def attend(queries, keys, values, allowed):
    scores = jnp.einsum("qhd,khd->hqk", queries, keys, preferred_element_type=jnp.float32)
    scores = jnp.where(allowed[None], scores, NEG)
    highest = jnp.max(scores, axis=2)
    expd = jnp.where(allowed[None], jnp.exp(scores - highest[:, :, None]), 0.0)
    totals = jnp.sum(expd, axis=2)
    weighted = jnp.einsum(
        "hqk,khd->qhd", expd.astype(jnp.bfloat16), values, preferred_element_type=jnp.float32
    )
    return (highest.T, totals.T, weighted)


def combine(first, second):
    highest = jnp.maximum(first[0], second[0])
    left_scale = jnp.exp(first[0] - highest)
    right_scale = jnp.exp(second[0] - highest)
    totals = first[1] * left_scale + second[1] * right_scale
    weighted = first[2] * left_scale[:, :, None] + second[2] * right_scale[:, :, None]
    return (highest, totals, weighted)


def window_mask(query_block, query_pos, key_block, key_pos, key_valid):
    near = (key_pos[None] < SINKS) | (key_pos[None] > query_pos[:, None] - WINDOW)
    same = key_block[None] == query_block[:, None]
    return key_valid[None] & same & (key_pos[None] <= query_pos[:, None]) & near


def key_meta(devices, pre_dev, pcb, span, first_off, second_off):
    stream = devices[:, None] * pre_dev + jnp.arange(pre_dev, dtype=jnp.int32)[None]
    new_block = stream // span
    new_pos = jnp.where(new_block == 0, first_off, second_off) + stream % span
    earlier = devices[:, None, None] * pcb + jnp.arange(pcb, dtype=jnp.int32)[None, :, None]
    old_block = jnp.zeros_like(earlier) + jnp.arange(2, dtype=jnp.int32)[None, None, :]
    old_pos = earlier + jnp.zeros_like(old_block)
    old_valid = old_pos < jnp.where(old_block == 0, first_off, second_off)
    count = devices.shape[0]
    key_block = jnp.concatenate([new_block, old_block.reshape(count, 2 * pcb)], axis=1).reshape(-1)
    key_pos = jnp.concatenate([new_pos, old_pos.reshape(count, 2 * pcb)], axis=1).reshape(-1)
    key_valid = jnp.concatenate(
        [jnp.ones((count, pre_dev), bool), old_valid.reshape(count, 2 * pcb)], axis=1
    ).reshape(-1)
    return (key_block, key_pos, key_valid)


def on_device(
    hidden,
    ln_gain,
    ln_bias,
    w_qkv,
    qkv_bias,
    w_out,
    out_bias,
    dec_cache,
    prior_kv,
    dec_len,
    offsets,
):
    tok_count = lax.axis_size("tok")
    my_index = lax.axis_index("tok")
    tok_rows = hidden.shape[0]
    dec_dev = dec_cache.shape[0]
    pre_dev = tok_rows - dec_dev
    lmax = dec_cache.shape[1]
    pcb = prior_kv.shape[0]
    head_width = w_qkv.shape[2]
    heads_dev = head_width // HEAD
    span = pre_dev * tok_count // 2
    first_off = offsets[0]
    second_off = offsets[1]
    inputs = hidden.astype(jnp.float32)
    average = jnp.mean(inputs, axis=1, keepdims=True)
    spread = jnp.mean((inputs - average) ** 2, axis=1, keepdims=True)
    normed = ((inputs - average) / jnp.sqrt(spread + 1e-05) * ln_gain + ln_bias).astype(
        jnp.bfloat16
    )
    feature_cols = lax.all_to_all(normed, "tok", split_axis=1, concat_axis=0, tiled=True)
    w_matrix = w_qkv.reshape(w_qkv.shape[0], 3 * head_width)
    summed = (
        lax.psum_scatter(
            jnp.dot(feature_cols, w_matrix, preferred_element_type=jnp.float32).astype(
                jnp.bfloat16
            ),
            "tok",
            scatter_dimension=0,
            tiled=True,
        )
        .astype(jnp.float32)
        .reshape(tok_rows, 3, head_width)
        + qkv_bias[None]
    )
    factors = jnp.array([HEAD ** (-0.5), 1.0, 1.0], jnp.float32)
    qkv = (summed * factors[None, :, None]).astype(jnp.bfloat16)
    new_kv = qkv[:, 1:]
    packed = jnp.concatenate(
        [
            qkv[:pre_dev, 1:].reshape(pre_dev, 2 * head_width),
            prior_kv.reshape(pcb * 2, 2 * head_width),
        ],
        axis=0,
    )
    per_device = pre_dev + 2 * pcb
    prefill_q = qkv[:pre_dev, 0]
    stream = my_index * pre_dev + jnp.arange(pre_dev, dtype=jnp.int32)
    query_block = stream // span
    query_pos = jnp.where(query_block == 0, first_off, second_off) + stream % span
    query_heads = prefill_q.reshape(pre_dev, heads_dev, HEAD)
    initial = (
        jnp.full((pre_dev, heads_dev), NEG, jnp.float32),
        jnp.zeros((pre_dev, heads_dev), jnp.float32),
        jnp.zeros((pre_dev, heads_dev, HEAD), jnp.float32),
    )
    piece = lax.all_gather(packed, "tok", axis=0, tiled=True)
    count = piece.shape[0] // per_device
    devices = jnp.arange(count, dtype=jnp.int32)
    key_block, fold_key_pos, key_valid = key_meta(
        devices, pre_dev, pcb, span, first_off, second_off
    )
    allowed = window_mask(query_block, query_pos, key_block, fold_key_pos, key_valid)
    key_heads = piece[:, :head_width].reshape(-1, heads_dev, HEAD)
    value_heads = piece[:, head_width:].reshape(-1, heads_dev, HEAD)
    final_state = combine(initial, attend(query_heads, key_heads, value_heads, allowed))
    prefill_out = final_state[2] / final_state[1][:, :, None]
    decode_rows = []
    for request in range(dec_dev):
        query = qkv[pre_dev + request, 0].reshape(1, heads_dev, HEAD)
        own_key = qkv[pre_dev + request, 1].reshape(1, heads_dev, HEAD)
        own_value = qkv[pre_dev + request, 2].reshape(1, heads_dev, HEAD)
        length = dec_len[request]
        cache = dec_cache[request]
        state = attend(query, own_key, own_value, jnp.ones((1, 1), bool))
        key_pos = jnp.arange(lmax, dtype=jnp.int32)
        visible = (key_pos < length) & ((key_pos < SINKS) | (key_pos > length - WINDOW))
        state = combine(
            state,
            attend(
                query,
                cache[:, 0].reshape(lmax, heads_dev, HEAD),
                cache[:, 1].reshape(lmax, heads_dev, HEAD),
                visible[None],
            ),
        )
        decode_rows.append(state[2][0] / state[1][0][:, None])
    decode_out = jnp.stack(decode_rows, axis=0)
    attn = jnp.concatenate(
        [prefill_out.reshape(pre_dev, head_width), decode_out.reshape(dec_dev, head_width)], axis=0
    ).astype(jnp.bfloat16)
    partial_rows = jnp.dot(
        lax.all_gather(attn, "tok", axis=0, tiled=True), w_out, preferred_element_type=jnp.float32
    )
    partial_value = lax.all_to_all(
        partial_rows.astype(jnp.bfloat16), "tok", split_axis=0, concat_axis=1, tiled=True
    ).astype(partial_rows.dtype)
    total = lax.psum(partial_value.astype(jnp.bfloat16), "tp").astype(jnp.float32)
    result = (inputs + total + out_bias).astype(jnp.bfloat16)
    return (result, new_kv)


def solution(mesh):
    in_specs = (
        P("tok", None),
        P(),
        P(),
        P("tok", None, "tp"),
        P(None, "tp"),
        P("tp", "tok"),
        P(),
        P("tok", None, None, "tp"),
        P("tok", None, None, "tp"),
        P("tok"),
        P(),
    )
    out_specs = (P("tok", None), P("tok", None, "tp"))
    return jax.shard_map(
        on_device, mesh=mesh, in_specs=in_specs, out_specs=out_specs, check_vma=False
    )
```

profile of v0, /device:TPU:2, one launch (start us, length us, event | category | flops | bytes accessed | tf_op | source)
XLA Modules:
  0.0 426.2 jit_solution(6795876849713984688)
XLA Ops:
  7.2 1.4 convert_reduce_fusion
  8.6 1.6 fusion.10
  10.2 1.6 fusion.13
  11.9 1.5 all_to_all.28
  13.3 1.6 copy.57
  14.9 7.6 %all-to-all-start = ((bf16[64,32,224]{2,0,1:T(8,128)(2,1)}), bf16[64,32,224]{2,0,1:T(8,128)(2,1)S(1)}, u32[]{:S(2)}, u32[]{:S(2)}) async-start(bf16[64,32,224]{2,0,1:T(8,128)(2,1)} %copy.57), calls=%async_computation | async-start | bytes 2097152 | tf_op jit(solution)/shard_map/all_to_all | solution.py:87
  22.6 1.8 copy.58
  24.4 12.5 %all-to-all-done = bf16[64,32,224]{2,0,1:T(8,128)(2,1)S(1)} async-done(((bf16[64,32,224]{2,0,1:T(8,128)(2,1)}), bf16[64,32,224]{2,0,1:T(8,128)(2,1)S(1)}, u32[]{:S(2)}, u32[]{:S(2)}) %all-to-all-start) | async-done | bytes 917536 | tf_op jit(solution)/shard_map/all_to_all | solution.py:87
  36.9 5.9 %convolution_convert_fusion = bf16[2048,2688]{1,0:T(8,128)(2,1)} fusion(bf16[2048,224]{1,0:T(8,128)(2,1)S(1)} %bitcast.162, bf16[224,2688]{0,1:T(8,128)(2,1)S(1)} %bitcast.166), kind=kOutput, calls=%fused_computation | convolution fusion | flops 2471755776 | bytes 13131776 | tf_op jit(solution)/shard_map/dot_general | solution.py:91
  42.9 0.8 copy-done.4
  43.8 107.7 %reduce-scatter.2.cloned.1.call-done = bf16[64,2688]{1,0:T(8,128)(2,1)} async-done(((bf16[2048,2688]{1,0:T(8,128)(2,1)}), bf16[64,2688]{1,0:T(8,128)(2,1)}) %reduce-scatter.2.cloned.1.call-update) | async-done | bytes 344080 | tf_op jit(solution)/shard_map/reduce_scatter | solution.py:90
  151.5 1.4 reshape.577
  152.9 0.3 multiply_convert_fusion
  153.2 0.2 slice.85
  153.4 0.2 pad.10
  153.6 0.8 maximum_bitcast_fusion
  154.4 0.2 all-gather.4.cloned.1.call-start
  154.7 7.7 %fusion.91 = (bf16[1,1024,2,896]{3,2,1,0:T(2,128)(2,1)}, bf16[1,1024,2,896]{3,2,1,0:T(2,128)(2,1)}) fusion(bf16[2,1024,2,896]{3,2,1,0:T(2,128)(2,1)} %param.19), kind=kLoop, calls=%fused_computation.144 | loop fusion | bytes 14680064 | tf_op jit(solution)/shard_map/slice | solution.py:140
  162.4 9.9 %copy.90 = bf16[1,1024,2,896]{1,3,2,0:T(8,128)(2,1)} copy(bf16[1,1024,2,896]{3,2,1,0:T(2,128)(2,1)} %get-tuple-element.19) | data formatting | bytes 7340032
  172.3 9.9 %copy.89 = bf16[1,1024,2,896]{1,3,2,0:T(8,128)(2,1)} copy(bf16[1,1024,2,896]{3,2,1,0:T(2,128)(2,1)} %get-tuple-element.18) | data formatting | bytes 7340032
  182.3 0.6 fusion.95
  184.5 0.7 fusion.94
  185.1 1.3 add_select_fusion.1
  186.5 0.1 le.19
  186.6 0.1 eq.47
  186.8 1.2 compare_select_fusion.1
  188.0 0.1 select_n.101
  188.2 0.1 copy.91
  188.3 0.1 and.78
  188.5 0.6 fusion.66
  189.1 0.7 fusion.65
  189.8 1.2 broadcast_add_fusion
  191.0 4.7 %fusion.93 = (bf16[1024,1,896]{0,2,1:T(8,128)(2,1)}, bf16[1024,1,896]{0,2,1:T(8,128)(2,1)}) fusion(bf16[1024,2,896]{0,2,1:T(8,128)(2,1)} %bitcast.157), kind=kLoop, calls=%fused_computation.146 | loop fusion | bytes 7340032 | tf_op jit(solution)/shard_map/slice | solution.py:149
  195.7 1.6 fusion.92
  197.3 0.4 or_and_fusion
  197.7 0.6 slice_reduce_fusion
  198.3 0.1 reshape_squeeze.10
  198.5 0.1 fusion.60
  198.7 2.2 fusion.69
  200.9 0.1 fusion.34
  201.0 1.9 fusion.71
  202.9 0.1 fusion.33
  203.1 0.2 fusion.44
  203.3 0.2 fusion.45
  203.6 0.6 fusion.35
  204.3 0.6 fusion.37
  205.0 13.3 %all-gather.6.cloned.1.call-done = bf16[32,94,1792]{2,1,0:T(8,128)(2,1)} async-done(((bf16[1,94,1792]{2,1,0:T(8,128)(2,1)}), bf16[32,94,1792]{2,1,0:T(8,128)(2,1)}) %all-gather.6.cloned.1.call-update) | async-done | bytes 10780688 | tf_op jit(solution)/shard_map/all_gather | solution.py:123
  218.3 11.3 %reshape.581 = bf16[3008,1792]{1,0:T(8,128)(2,1)} reshape(bf16[32,94,1792]{2,1,0:T(8,128)(2,1)} %all-gather.6.cloned.1.call-done) | data formatting | bytes 21561344
  229.5 9.1 %fusion.90 = (bf16[3008,896]{1,0:T(8,128)(2,1)}, bf16[3008,896]{1,0:T(8,128)(2,1)}) fusion(bf16[3008,1792]{1,0:T(8,128)(2,1)} %reshape.581), kind=kLoop, calls=%fused_computation.143 | loop fusion | bytes 21561344 | tf_op jit(solution)/shard_map/slice | solution.py:130
  238.6 8.3 %copy.62 = bf16[3008,896]{0,1:T(8,128)(2,1)} copy(bf16[3008,896]{1,0:T(8,128)(2,1)} %get-tuple-element.17) | data formatting | bytes 10780672 | tf_op jit(solution)/shard_map/slice | solution.py:131
  246.9 8.3 %copy.59 = bf16[3008,896]{0,1:T(8,128)(2,1)} copy(bf16[3008,896]{1,0:T(8,128)(2,1)} %get-tuple-element.16) | data formatting | bytes 10780672 | tf_op jit(solution)/shard_map/slice | solution.py:130
  255.2 4.2 select_reduce_fusion
  259.4 1.5 fusion
  260.9 2.2 fusion.28
  263.3 0.7 pad_maximum_fusion
  264.1 50.0 %all-gather.4.cloned.1.call-done = bf16[2048,896]{1,0:T(8,128)(2,1)} async-done(((bf16[64,896]{1,0:T(8,128)(2,1)}), bf16[2048,896]{1,0:T(8,128)(2,1)}) %all-gather.4.cloned.1.call-update) | async-done | bytes 3670032 | tf_op jit(solution)/shard_map/all_gather | solution.py:159
  314.0 3.4 convolution_convert_fusion.1
  317.4 0.5 copy.67
  317.9 20.2 %all_to_all.38 = bf16[32,64,224]{2,1,0:T(8,128)(2,1)S(1)} all-to-all(bf16[32,64,224]{2,1,0:T(8,128)(2,1)S(1)} %bitcast.168), channel_id=1, replica_groups=mesh['tok'=32,'tp'=8] {'tok'}, dimensions={0} | all-to-all | bytes 1835008 | tf_op jit(solution)/shard_map/all_to_all | solution.py:161
  338.2 0.6 copy.68
  338.7 2.8 all_to_all.35
  341.6 0.9 slice.98
  342.5 74.7 %all-reduce.3.cloned.1.call-done = bf16[64,7168]{1,0:T(8,128)(2,1)} async-done(((bf16[64,7168]{1,0:T(8,128)(2,1)}), bf16[64,7168]{1,0:T(8,128)(2,1)}) %all-reduce.3.cloned.1.call-update) | async-done | bytes 917520 | tf_op jit(solution)/shard_map/psum | solution.py:164
  417.3 2.4 fusion.15
  (62 shorter events, 1.4 us)
Async XLA Ops:
  7.2 306.9 %copy-start = (bf16[896,224]{0,1:T(8,128)(2,1)S(1)}, bf16[896,224]{0,1:T(8,128)(2,1)}, u32[]{:S(2)}) copy-start(bf16[896,224]{0,1:T(8,128)(2,1)} %param.17) | copy-start | bytes 1204228
  14.9 22.0 %all-to-all-start = ((bf16[64,32,224]{2,0,1:T(8,128)(2,1)}), bf16[64,32,224]{2,0,1:T(8,128)(2,1)S(1)}, u32[]{:S(2)}, u32[]{:S(2)}) async-start(bf16[64,32,224]{2,0,1:T(8,128)(2,1)} %copy.57), calls=%async_computation | async-start | bytes 2097152 | tf_op jit(solution)/shard_map/all_to_all | solution.py:87
  22.5 128.9 %reduce-scatter.2.cloned.1.call-start = ((), (), s32[]{:S(2)}) async-start(), calls=%async_computation.3 | async-start | bytes 11354112 | tf_op jit(solution)/shard_map/reduce_scatter | solution.py:90
  42.8 0.9 copy-start.4
  42.8 110.0 %copy-start.6 = (f32[3,896]{1,0:T(4,128)S(1)}, f32[3,896]{1,0:T(4,128)}, u32[]{:S(2)}) copy-start(f32[3,896]{1,0:T(4,128)} %param.16) | copy-start | bytes 32260
  42.8 110.0 %copy-start.9 = (f32[3]{0:T(128)S(1)}, f32[3]{0:T(128)}, u32[]{:S(2)}) copy-start(f32[3]{0:T(128)} %constant.75.clone) | copy-start | bytes 40
  42.9 175.4 %all-gather.6.cloned.1.call-start = ((), (), s32[]{:S(2)}) async-start(), calls=%async_computation.6 | async-start | bytes 11354112 | tf_op jit(solution)/shard_map/all_gather | solution.py:123
  154.4 159.6 %all-gather.4.cloned.1.call-start = ((), (), s32[]{:S(2)}) async-start(), calls=%async_computation.4 | async-start | bytes 3784704 | tf_op jit(solution)/shard_map/all_gather | solution.py:159
  172.3 9.9 %copy-start.7 = (s32[2]{0:T(128)S(1)}, s32[2]{0:T(128)}, u32[]{:S(2)}) copy-start(s32[2]{0:T(128)} %param.21) | copy-start | bytes 28
  172.3 12.2 %copy-start.8 = (s32[2]{0:T(128)S(1)}, s32[2]{0:T(128)}, u32[]{:S(2)}) copy-start(s32[2]{0:T(128)} %param.22) | copy-start | bytes 28
  191.0 4.7 %copy-start.1 = (bf16[1,1024,2,896]{1,3,2,0:T(8,128)(2,1)S(1)}, bf16[1,1024,2,896]{1,3,2,0:T(8,128)(2,1)}, u32[]{:S(2)}) copy-start(bf16[1,1024,2,896]{1,3,2,0:T(8,128)(2,1)} %copy.89) | copy-start | bytes 11010052
  198.5 5.2 %copy-start.3 = (bf16[1024,1,896]{0,2,1:T(8,128)(2,1)S(1)}, bf16[1024,1,896]{0,2,1:T(8,128)(2,1)}, u32[]{:S(2)}) copy-start(bf16[1024,1,896]{0,2,1:T(8,128)(2,1)} %get-tuple-element.22) | copy-start | bytes 5505028
  255.2 5.8 %slice-start = ((s8[5505024]{0:T(1024)(128)(4,1)}), s8[4194304]{0:T(1024)(128)(4,1)S(1)}, s32[]{:S(2)}) async-start(s8[5505024]{0:T(1024)(128)(4,1)} %bitcast.163), calls=%async_computation.7 | async-start | bytes 8388608
  255.2 5.8 %slice-start.1 = ((s8[5505024]{0:T(1024)(128)(4,1)}), s8[1310720]{0:T(1024)(128)(4,1)S(1)}, s32[]{:S(2)}) async-start(s8[5505024]{0:T(1024)(128)(4,1)} %bitcast.163), calls=%async_computation.8 | async-start | bytes 2621440
  264.0 153.2 %all-reduce.3.cloned.1.call-start = ((), (), s32[]{:S(2)}) async-start(), calls=%async_computation.5 | async-start | bytes 1835008 | tf_op jit(solution)/shard_map/psum | solution.py:164
  317.9 99.3 %copy-start.2 = (bf16[64,7168]{1,0:T(8,128)(2,1)S(1)}, bf16[64,7168]{1,0:T(8,128)(2,1)}, u32[]{:S(2)}) copy-start(bf16[64,7168]{1,0:T(8,128)(2,1)} %param.12) | copy-start | bytes 2752516
  317.9 99.3 %copy-start.5 = (f32[7168]{0:T(1024)S(1)}, f32[7168]{0:T(1024)}, u32[]{:S(2)}) copy-start(f32[7168]{0:T(1024)} %param.18) | copy-start | bytes 86020
Sparse Core Ops, SparseCore 0:
  43.0 108.4 reduce-scatter.1
  154.6 63.6 all-gather.5
  264.1 49.8 all-gather.3
  341.7 75.4 all-reduce.2
where the time goes:
time: 428 us; the launch traced here: 426 us
  waiting for transfers between devices  258 us (60%)
  local copies, waits for them, and re-layouts  86.4 us (20%)
  matrix products  20.9 us (5%)
  blocking collectives  20.2 us (5%)
  other arithmetic  17 us (4%)
  between operations  15.4 us (4%)
  starting transfers between devices  7.97 us (2%)
    reduce_scatter x1, waiting for transfers between devices, on_device(): lax.psum_scatter(jnp.dot(feature_cols, w_matrix, preferred_element_type=j...  108 us
    psum x1, waiting for transfers between devices, on_device(): lax.psum(partial_value.astype(jnp.bfloat16), 'tp').astype(jnp.float32)  74.7 us
    all_gather x1, waiting for transfers between devices, on_device(): lax.all_gather(attn, 'tok', axis=0, tiled=True)  50 us
    unnamed x36, local copies, waits for them, and re-layouts  34.3 us
    all_to_all x1, blocking collectives, on_device(): lax.all_to_all(partial_rows.astype(jnp.bfloat16), 'tok', split_axis=0, co...  20.2 us
    slice x2, local copies, waits for them, and re-layouts, on_device(): key_heads = piece[:, :head_width].reshape(-1, heads_dev, HEAD)  17.4 us
    all_gather x1, waiting for transfers between devices, on_device(): piece = lax.all_gather(packed, 'tok', axis=0, tiled=True)  13.3 us
    all_to_all x1, waiting for transfers between devices, on_device(): lax.all_to_all(normed, 'tok', split_axis=1, concat_axis=0, tiled=True)  12.5 us
  transfers between devices with their start and end apart: 5, of which 5 were waited for; matrix products, arithmetic and copies ran while one was open for 12% of the time, Pallas kernels for 0%

commit v1 on v0

--- a/solution.py
+++ b/solution.py
@@ -84,7 +84,10 @@
     normed = ((inputs - average) / jnp.sqrt(spread + 1e-05) * ln_gain + ln_bias).astype(
         jnp.bfloat16
     )
-    feature_cols = lax.all_to_all(normed, "tok", split_axis=1, concat_axis=0, tiled=True)
+    feature_cols = jnp.concatenate(
+        lax.all_to_all(jnp.stack(jnp.split(normed, lax.axis_size("tok"), axis=1)), "tok", 0, 0),
+        axis=0,
+    )
     w_matrix = w_qkv.reshape(w_qkv.shape[0], 3 * head_width)
     summed = (
         lax.psum_scatter(

time: 428 us -> 453 us (1.058)
  local copies, waits for them, and re-layouts: 86.4 us -> 107 us
    unnamed x36 -> x65, local copies, waits for them, and re-layouts: 34.3 us -> 57.2 us
where the time goes in v1:
time: 453 us; the launch traced here: 451 us
  waiting for transfers between devices  258 us (57%)
  local copies, waits for them, and re-layouts  107 us (24%)
  matrix products  25 us (6%)
  blocking collectives  20.2 us (4%)
  other arithmetic  17.3 us (4%)
  between operations  15.4 us (3%)
  starting transfers between devices  8.01 us (2%)
    reduce_scatter x1, waiting for transfers between devices, on_device(): lax.psum_scatter(jnp.dot(feature_cols, w_matrix, preferred_element_type=j...  108 us
    psum x1, waiting for transfers between devices, on_device(): lax.psum(partial_value.astype(jnp.bfloat16), 'tp').astype(jnp.float32)  74.7 us
    unnamed x65, local copies, waits for them, and re-layouts  57.2 us
    all_gather x1, waiting for transfers between devices, on_device(): lax.all_gather(attn, 'tok', axis=0, tiled=True)  49.7 us
    all_to_all x1, blocking collectives, on_device(): lax.all_to_all(partial_rows.astype(jnp.bfloat16), 'tok', split_axis=0, co...  20.2 us
    slice x2, local copies, waits for them, and re-layouts, on_device(): key_heads = piece[:, :head_width].reshape(-1, heads_dev, HEAD)  17.2 us
    all_gather x1, waiting for transfers between devices, on_device(): piece = lax.all_gather(packed, 'tok', axis=0, tiled=True)  13.2 us
    all_to_all x1, waiting for transfers between devices, on_device(): lax.all_to_all(jnp.stack(jnp.split(normed, lax.axis_size('tok'), axis=1))...  12.5 us
  transfers between devices with their start and end apart: 5, of which 5 were waited for; matrix products, arithmetic and copies ran while one was open for 12% of the time, Pallas kernels for 0%

profile of v1, /device:TPU:2, one launch (start us, length us, event | category | flops | bytes accessed | tf_op | source)
XLA Modules:
  0.0 450.7 jit_solution(14022703478107662442)
XLA Ops:
  7.2 1.4 convert_reduce_fusion
  8.6 1.6 fusion.10
  10.2 1.6 fusion.13
  12.5 0.7 constant_dynamic-update-slice_fusion.30
  13.2 0.7 constant_dynamic-update-slice_fusion.29
  13.8 0.7 constant_dynamic-update-slice_fusion.28
  15.1 0.7 constant_dynamic-update-slice_fusion.26
  15.8 0.7 constant_dynamic-update-slice_fusion.25
  16.5 0.7 constant_dynamic-update-slice_fusion.24
  17.8 0.7 constant_dynamic-update-slice_fusion.22
  18.5 0.7 constant_dynamic-update-slice_fusion.21
  19.2 0.7 constant_dynamic-update-slice_fusion.20
  20.5 0.7 constant_dynamic-update-slice_fusion.18
  21.1 0.7 constant_dynamic-update-slice_fusion.17
  21.8 0.7 constant_dynamic-update-slice_fusion.16
  23.1 0.7 constant_dynamic-update-slice_fusion.14
  23.8 0.7 constant_dynamic-update-slice_fusion.13
  24.5 0.7 constant_dynamic-update-slice_fusion.12
  25.8 0.7 constant_dynamic-update-slice_fusion.10
  26.5 0.7 constant_dynamic-update-slice_fusion.9
  27.1 0.7 constant_dynamic-update-slice_fusion.8
  28.4 0.7 constant_dynamic-update-slice_fusion.6
  29.1 0.7 constant_dynamic-update-slice_fusion.5
  29.8 0.7 constant_dynamic-update-slice_fusion.4
  31.1 0.7 constant_dynamic-update-slice_fusion.2
  31.8 0.7 constant_dynamic-update-slice_fusion.1
  32.5 0.7 constant_dynamic-update-slice_fusion
  33.2 7.6 %all-to-all-start = ((bf16[32,64,224]{2,1,0:T(8,128)(2,1)}), bf16[32,64,224]{2,1,0:T(8,128)(2,1)S(1)}, u32[]{:S(2)}, u32[]{:S(2)}) async-start(bf16[32,64,224]{2,1,0:T(8,128)(2,1)} %constant_dynamic-update-slice_fusion), calls=%async_computation | async-start | bytes 2097152 | tf_op jit(solution)/shard_map/all_to_all | solution.py:88
  40.8 1.8 copy.54
  42.7 12.5 %all-to-all-done = bf16[32,64,224]{2,1,0:T(8,128)(2,1)S(1)} async-done(((bf16[32,64,224]{2,1,0:T(8,128)(2,1)}), bf16[32,64,224]{2,1,0:T(8,128)(2,1)S(1)}, u32[]{:S(2)}, u32[]{:S(2)}) %all-to-all-start) | async-done | bytes 917536 | tf_op jit(solution)/shard_map/all_to_all | solution.py:88
  55.2 5.9 %convolution_convert_fusion = bf16[2048,2688]{1,0:T(8,128)(2,1)} fusion(bf16[2048,224]{1,0:T(8,128)(2,1)S(1)} %bitcast.288, bf16[224,2688]{0,1:T(8,128)(2,1)S(1)} %bitcast.290), kind=kOutput, calls=%fused_computation | convolution fusion | flops 2471755776 | bytes 13131776 | tf_op jit(solution)/shard_map/dot_general | solution.py:94
  61.2 0.8 copy-done.5
  62.0 107.7 %reduce-scatter.2.cloned.1.call-done = bf16[64,2688]{1,0:T(8,128)(2,1)} async-done(((bf16[2048,2688]{1,0:T(8,128)(2,1)}), bf16[64,2688]{1,0:T(8,128)(2,1)}) %reduce-scatter.2.cloned.1.call-update) | async-done | bytes 344080 | tf_op jit(solution)/shard_map/reduce_scatter | solution.py:93
  169.7 1.4 reshape.578
  171.9 0.8 maximum_bitcast_fusion
  173.0 0.7 fusion.94
  173.7 1.4 add_select_fusion.1
  175.4 1.3 compare_select_fusion.1
  177.2 7.9 %fusion.91 = (bf16[1,1024,2,896]{3,2,1,0:T(2,128)(2,1)}, bf16[1,1024,2,896]{3,2,1,0:T(2,128)(2,1)}) fusion(bf16[2,1024,2,896]{3,2,1,0:T(2,128)(2,1)} %param.19), kind=kLoop, calls=%fused_computation.208 | loop fusion | bytes 14680064 | tf_op jit(solution)/shard_map/slice | solution.py:143
  185.2 9.9 %copy.85 = bf16[1,1024,2,896]{1,3,2,0:T(8,128)(2,1)} copy(bf16[1,1024,2,896]{3,2,1,0:T(2,128)(2,1)} %get-tuple-element.18) | data formatting | bytes 7340032
  195.0 10.0 %copy.86 = bf16[1,1024,2,896]{1,3,2,0:T(8,128)(2,1)} copy(bf16[1,1024,2,896]{3,2,1,0:T(2,128)(2,1)} %get-tuple-element.19) | data formatting | bytes 7340032
  206.9 0.7 fusion.65
  208.2 1.3 broadcast_add_fusion
  209.6 4.4 fusion.92
  214.0 1.6 fusion.93
  217.0 2.2 fusion.71
  219.3 1.9 fusion.69
  223.3 13.2 %all-gather.6.cloned.1.call-done = bf16[32,94,1792]{2,1,0:T(8,128)(2,1)} async-done(((bf16[1,94,1792]{2,1,0:T(8,128)(2,1)}), bf16[32,94,1792]{2,1,0:T(8,128)(2,1)}) %all-gather.6.cloned.1.call-update) | async-done | bytes 10780688 | tf_op jit(solution)/shard_map/all_gather | solution.py:126
  236.5 11.3 %reshape.582 = bf16[3008,1792]{1,0:T(8,128)(2,1)} reshape(bf16[32,94,1792]{2,1,0:T(8,128)(2,1)} %all-gather.6.cloned.1.call-done) | data formatting | bytes 21561344
  247.8 9.0 %fusion.90 = (bf16[3008,896]{1,0:T(8,128)(2,1)}, bf16[3008,896]{1,0:T(8,128)(2,1)}) fusion(bf16[3008,1792]{1,0:T(8,128)(2,1)} %reshape.582), kind=kLoop, calls=%fused_computation.207 | loop fusion | bytes 21561344 | tf_op jit(solution)/shard_map/slice | solution.py:133
  256.8 8.3 %copy.55 = bf16[3008,896]{0,1:T(8,128)(2,1)} copy(bf16[3008,896]{1,0:T(8,128)(2,1)} %get-tuple-element.16) | data formatting | bytes 10780672 | tf_op jit(solution)/shard_map/slice | solution.py:133
  265.0 4.1 select_reduce_fusion
  269.1 2.4 copy-done.1
  271.5 1.5 fusion
  273.0 8.3 %copy.58 = bf16[3008,896]{0,1:T(8,128)(2,1)} copy(bf16[3008,896]{1,0:T(8,128)(2,1)} %get-tuple-element.17) | data formatting | bytes 10780672 | tf_op jit(solution)/shard_map/slice | solution.py:134
  281.3 6.4 %fusion.28 = bf16[62,7,128]{2,0,1:T(8,128)(2,1)S(1)} fusion(bf16[3008,7,128]{0,2,1:T(8,128)(2,1)} %bitcast.289, f32[7,62,3008]{2,1,0:T(8,128)} %copy-done.1, f32[7,62]{1,0:T(8,128)S(1)} %get-tuple-element.39, pred[62,3008]{1,0:T(8,128)(4,1)S(1)} %or_and_fusion, f32[62,7]{0,1:T(8,128)S(1)} %get-tuple-element.29, f32[62,7]{0,1:T(8,128)S(1)} %get-tuple-element.30, ...), kind=kOutput, calls=%fused_computation.26 | convolution fusion | flops 339644928 | bytes 10916768 | tf_op jit(solution)/shard_map/hqk,khd->qhd/dot_general | solution.py:18
  287.8 0.7 pad_maximum_fusion
  288.8 49.7 %all-gather.4.cloned.1.call-done = bf16[2048,896]{1,0:T(8,128)(2,1)} async-done(((bf16[64,896]{1,0:T(8,128)(2,1)}), bf16[2048,896]{1,0:T(8,128)(2,1)}) %all-gather.4.cloned.1.call-update) | async-done | bytes 3670032 | tf_op jit(solution)/shard_map/all_gather | solution.py:162
  338.6 3.4 convolution_convert_fusion.1
  342.5 20.2 %all_to_all.24 = bf16[32,64,224]{2,1,0:T(8,128)(2,1)S(1)} all-to-all(bf16[32,64,224]{2,1,0:T(8,128)(2,1)S(1)} %bitcast.292), channel_id=1, replica_groups=mesh['tok'=32,'tp'=8] {'tok'}, dimensions={0} | all-to-all | bytes 1835008 | tf_op jit(solution)/shard_map/all_to_all | solution.py:164
  363.3 2.8 all_to_all.21
  366.1 0.9 slice.98
  367.0 74.7 %all-reduce.3.cloned.1.call-done = bf16[64,7168]{1,0:T(8,128)(2,1)} async-done(((bf16[64,7168]{1,0:T(8,128)(2,1)}), bf16[64,7168]{1,0:T(8,128)(2,1)}) %all-reduce.3.cloned.1.call-update) | async-done | bytes 917520 | tf_op jit(solution)/shard_map/psum | solution.py:167
  441.8 2.4 fusion.15
  (89 shorter events, 13.1 us)
Async XLA Ops:
  7.2 331.4 %copy-start = (bf16[896,224]{0,1:T(8,128)(2,1)S(1)}, bf16[896,224]{0,1:T(8,128)(2,1)}, u32[]{:S(2)}) copy-start(bf16[896,224]{0,1:T(8,128)(2,1)} %param.17) | copy-start | bytes 1204228
  33.2 22.0 %all-to-all-start = ((bf16[32,64,224]{2,1,0:T(8,128)(2,1)}), bf16[32,64,224]{2,1,0:T(8,128)(2,1)S(1)}, u32[]{:S(2)}, u32[]{:S(2)}) async-start(bf16[32,64,224]{2,1,0:T(8,128)(2,1)} %constant_dynamic-update-slice_fusion), calls=%async_computation | async-start | bytes 2097152 | tf_op jit(solution)/shard_map/all_to_all | solution.py:88
  40.8 128.9 %reduce-scatter.2.cloned.1.call-start = ((), (), s32[]{:S(2)}) async-start(), calls=%async_computation.3 | async-start | bytes 11354112 | tf_op jit(solution)/shard_map/reduce_scatter | solution.py:93
  61.1 0.9 copy-start.5
  61.1 110.0 %copy-start.7 = (f32[3,896]{1,0:T(4,128)S(1)}, f32[3,896]{1,0:T(4,128)}, u32[]{:S(2)}) copy-start(f32[3,896]{1,0:T(4,128)} %param.16) | copy-start | bytes 32260
  61.1 110.0 %copy-start.10 = (f32[3]{0:T(128)S(1)}, f32[3]{0:T(128)}, u32[]{:S(2)}) copy-start(f32[3]{0:T(128)} %constant.75.clone) | copy-start | bytes 40
  61.1 111.9 %copy-start.8 = (s32[2]{0:T(128)S(1)}, s32[2]{0:T(128)}, u32[]{:S(2)}) copy-start(s32[2]{0:T(128)} %param.22) | copy-start | bytes 28
  61.1 175.4 %all-gather.6.cloned.1.call-start = ((), (), s32[]{:S(2)}) async-start(), calls=%async_computation.6 | async-start | bytes 11354112 | tf_op jit(solution)/shard_map/all_gather | solution.py:126
  172.7 165.9 %all-gather.4.cloned.1.call-start = ((), (), s32[]{:S(2)}) async-start(), calls=%async_computation.4 | async-start | bytes 3784704 | tf_op jit(solution)/shard_map/all_gather | solution.py:162
  195.0 10.0 %copy-start.9 = (s32[2]{0:T(128)S(1)}, s32[2]{0:T(128)}, u32[]{:S(2)}) copy-start(s32[2]{0:T(128)} %param.21) | copy-start | bytes 28
  209.6 4.4 copy-start.2
  216.8 5.2 %copy-start.4 = (bf16[1024,1,896]{0,2,1:T(8,128)(2,1)S(1)}, bf16[1024,1,896]{0,2,1:T(8,128)(2,1)}, u32[]{:S(2)}) copy-start(bf16[1024,1,896]{0,2,1:T(8,128)(2,1)} %get-tuple-element.20) | copy-start | bytes 5505028
  269.1 2.4 copy-start.1
  288.5 153.2 %all-reduce.3.cloned.1.call-start = ((), (), s32[]{:S(2)}) async-start(), calls=%async_computation.5 | async-start | bytes 1835008 | tf_op jit(solution)/shard_map/psum | solution.py:167
  342.5 99.3 %copy-start.3 = (bf16[64,7168]{1,0:T(8,128)(2,1)S(1)}, bf16[64,7168]{1,0:T(8,128)(2,1)}, u32[]{:S(2)}) copy-start(bf16[64,7168]{1,0:T(8,128)(2,1)} %param.12) | copy-start | bytes 2752516
  342.5 99.3 %copy-start.6 = (f32[7168]{0:T(1024)S(1)}, f32[7168]{0:T(1024)}, u32[]{:S(2)}) copy-start(f32[7168]{0:T(1024)} %param.18) | copy-start | bytes 86020
Sparse Core Ops, SparseCore 0:
  61.2 108.4 reduce-scatter.1
  172.8 63.6 all-gather.5
  288.7 49.8 all-gather.3
  366.2 75.4 all-reduce.2
